TPU v7x, 32 devices: a whole 2x2x4 slice. The times are simulated.
32 devices in a mesh: slab: 16 (over z, x, core), vec: 2 (over y).
Axes of the slice: x: 2, y: 2, z: 4, core: 2. Of those that a mesh axis runs over, the one named last changes fastest.
Arguments:
- block: bfloat16 [64, 3, 16, 16, 128], P('vec', None, 'slab'), may hold values from -8 to 8
- labels: int32 [16, 16, 128], P('slab'), may hold values from 0 to 3
- flags: int32 [16, 16, 128], P('slab'), may hold values 0 or 1
- stiffness: float32 [4], replicated, may hold values from 0.25 to 2.5
- density: float32 [4], replicated, may hold values from 0.5 to 4
Outputs:
- filtered: bfloat16 [64, 3, 16, 16, 128], P('vec', None, 'slab')
- gram: float32 [64, 64], P('vec')
Inputs may be any that keep to these rules, and one draw needn't show every extreme that they name: `labels`: 0 steel, 1 weld, 2 bearing, 3 void filler.
All inputs are finite; a program needn't handle non-finite values. No bound on the sum of `flags` on one device may be relied on, other than what follows from the above.
Results may differ from a plain program's by a relative error of at most 0.0049.
Values may be sent and summed in bfloat16 or wider, within the bound.
A program may use at most 64 MiB of HBM per device.

v0:
```python
import jax
import jax.numpy as jnp
from jax import lax
from jax.sharding import PartitionSpec as P

axial_modulus = 0.75
shear_modulus = 0.25
dilation_modulus = 0.5


def padded_2(block, sides, width):
    for axis, dim in sides:
        count = lax.axis_size(axis)
        forward = [(i, i + 1) for i in range(count - 1)]
        backward = [(target, source) for source, target in forward]
        low = lax.ppermute(
            lax.slice_in_dim(block, block.shape[dim] - width, None, axis=dim), axis, forward
        )
        high = lax.ppermute(lax.slice_in_dim(block, 0, width, axis=dim), axis, backward)
        block = jnp.concatenate([low, block, high], axis=dim)
    return block


def lookup_table(table, labels):
    summed = jnp.zeros(labels.shape, jnp.float32)
    for material in range(table.shape[0]):
        summed = summed + jnp.where(labels == material, table[material], jnp.float32(0.0))
    return summed


def stencil_pass(values, axis_index, operation):
    length = values.shape[axis_index] - 2
    lower = lax.slice_in_dim(values, 0, length, axis=axis_index)
    middle = lax.slice_in_dim(values, 1, length + 1, axis=axis_index)
    higher = lax.slice_in_dim(values, 2, length + 2, axis=axis_index)
    if operation == "avg":
        return (lower + 4.0 * middle + higher) / 6.0
    if operation == "second":
        return lower - 2.0 * middle + higher
    return (higher - lower) * 0.5


def separable(values, operations):
    for position in range(3):
        values = stencil_pass(values, position + 1, operations[position])
    return values


def navier(padded):
    components = [padded[:, source] for source in range(3)]
    results = []
    for target in range(3):
        summed = 0.0
        for direction in range(3):
            operations = ["avg", "avg", "avg"]
            operations[direction] = "second"
            factor = axial_modulus if direction == target else shear_modulus
            summed = summed - factor * separable(components[target], operations)
        for source in range(3):
            if source != target:
                operations = ["avg", "avg", "avg"]
                operations[target] = "first"
                operations[source] = "first"
                summed = summed - dilation_modulus * separable(components[source], operations)
        results.append(summed)
    return jnp.stack(results, axis=1)


def shards(block, labels, flags, stiffness, density):
    gain = jnp.sqrt(lookup_table(stiffness, labels)) * (1 - flags).astype(jnp.float32)
    mass = lookup_table(density, labels)
    scaled = (gain * block.astype(jnp.float32)).astype(jnp.bfloat16)
    padded = padded_2(scaled, (("slab", 2),), 1)
    padded = jnp.pad(padded.astype(jnp.float32), ((0, 0), (0, 0), (0, 0), (1, 1), (1, 1)))
    summed = navier(padded)
    filtered = (gain * summed).astype(jnp.bfloat16)
    rows_flat = filtered.reshape(
        filtered.shape[0], 3, filtered.shape[2] * filtered.shape[3], filtered.shape[4]
    )
    gathered = lax.all_to_all(rows_flat, "vec", split_axis=2, concat_axis=0, tiled=True)
    vec_count = gathered.shape[0]
    group_count = filtered.shape[0]
    share_rows = gathered.shape[2]
    mass_rows = mass.reshape(-1, mass.shape[2])
    mass_share = lax.dynamic_slice_in_dim(
        mass_rows, lax.axis_index("vec") * share_rows, share_rows, 0
    )
    weighted = (mass_share * gathered.astype(jnp.float32)).astype(jnp.bfloat16)
    partial_gram = lax.dot_general(
        gathered.reshape(vec_count, -1),
        weighted.reshape(vec_count, -1),
        (((1,), (1,)), ((), ())),
        preferred_element_type=jnp.float32,
    )
    unknowns = 3 * filtered.shape[2] * lax.axis_size("slab") * filtered.shape[3] * filtered.shape[4]
    summed_gram = lax.psum(partial_gram, ("slab", "vec"))
    row_block = lax.dynamic_slice_in_dim(
        summed_gram, lax.axis_index("vec") * group_count, group_count, 0
    )
    gram = row_block / jnp.float32(unknowns)
    return (filtered, gram)


def solution(mesh):
    in_specs = (
        P("vec", None, "slab", None, None),
        P("slab", None, None),
        P("slab", None, None),
        P(),
        P(),
    )
    out_specs = (P("vec", None, "slab", None, None), P("vec", None))
    return jax.shard_map(shards, mesh=mesh, in_specs=in_specs, out_specs=out_specs, check_vma=False)
```

profile of v0, /device:TPU:0, one launch (start us, length us, event | category | flops | bytes accessed | tf_op | source)
XLA Modules:
  0.0 80.2 jit_solution(18236181936846677165)
XLA Ops:
  0.6 1.5 %fusion.65 = (f32[1]{0:T(128)}, f32[1]{0:T(128)}, f32[1]{0:T(128)}, f32[1]{0:T(128)}) fusion(f32[4]{0:T(128)} %param.8), kind=kLoop, calls=%fused_computation.140 | loop fusion | bytes 32 | tf_op jit(solution)/shard_map/slice | solution.py:27
  2.1 3.3 %multiply_bitcast_fusion = (f32[16,128]{1,0:T(8,128)S(1)}, pred[1,16,128]{2,1,0:T(8,128)(4,1)S(1)}, pred[1,16,128]{2,1,0:T(8,128)(4,1)S(1)}, pred[1,16,128]{2,1,0:T(8,128)(4,1)S(1)}, pred[1,16,128]{2,1,0:T(8,128)(4,1)S(1)}) fusion(s32[1,16,128]{2,1,0:T(8,128)} %param.7, f32[]{:T(128)} %bitcast.3, f32[]{:T(128)} %bitcast.2, f32[]{:T(128)} %bitcast.1, ...), kind=kLoop, calls=%fused_computation.133 | loop fusion | flops 28672 | bytes 32784 | tf_op jit(solution)/shard_map/mul | solution.py:76
  5.4 1.1 %multiply_convert_fusion.1 = bf16[32,3,1,16,128]{4,0,3,2,1:T(8,128)(2,1)S(1)} fusion(bf16[32,3,1,16,128]{4,3,2,1,0:T(8,128)(2,1)} %param.5, f32[16,128]{1,0:T(8,128)S(1)} %get-tuple-element.4), kind=kLoop, calls=%fused_computation.21 | loop fusion | flops 589824 | bytes 794624 | tf_op jit(solution)/shard_map/convert_element_type | solution.py:72
  6.5 1.3 %collective-permute-start.1 = (bf16[32,3,1,16,128]{4,0,3,2,1:T(8,128)(2,1)S(1)}, bf16[32,3,1,16,128]{4,0,3,2,1:T(8,128)(2,1)S(1)}, u32[]{:S(2)}, u32[]{:S(2)}) collective-permute-start(bf16[32,3,1,16,128]{4,0,3,2,1:T(8,128)(2,1)S(1)} %multiply_convert_fusion.1), channel_id=1, source_target_pairs={{2,0},{4,2},{6,4},{8,6},{10,8},{12,10},{14,12},{16,14},{18,16},{20... | collective-permute-start | bytes 1179656 | tf_op jit(solution)/shard_map/ppermute | solution.py:19
  7.8 3.1 %collective-permute-start = (bf16[32,3,1,16,128]{4,0,3,2,1:T(8,128)(2,1)S(1)}, bf16[32,3,1,16,128]{4,0,3,2,1:T(8,128)(2,1)S(1)}, u32[]{:S(2)}, u32[]{:S(2)}) collective-permute-start(bf16[32,3,1,16,128]{4,0,3,2,1:T(8,128)(2,1)S(1)} %multiply_convert_fusion.1), channel_id=1, source_target_pairs={{0,2},{2,4},{4,6},{6,8},{8,10},{10,12},{12,14},{14,16},{16,18},{18... | collective-permute-start | bytes 1179656 | tf_op jit(solution)/shard_map/ppermute | solution.py:16
  10.8 1.5 %fusion.64 = (f32[1]{0:T(128)}, f32[1]{0:T(128)}, f32[1]{0:T(128)}, f32[1]{0:T(128)}) fusion(f32[4]{0:T(128)} %param.9), kind=kLoop, calls=%fused_computation.139 | loop fusion | bytes 32 | tf_op jit(solution)/shard_map/slice | solution.py:27
  12.3 2.6 %add_bitcast_fusion = f32[8,128]{1,0:T(8,128)S(1)} fusion(pred[1,16,128]{2,1,0:T(8,128)(4,1)S(1)} %get-tuple-element.8, s32[]{:T(128)S(6)} %select_n.39, pred[1,16,128]{2,1,0:T(8,128)(4,1)S(1)} %get-tuple-element.7, pred[1,16,128]{2,1,0:T(8,128)(4,1)S(1)} %get-tuple-element.6, pred[1,16,128]{2,1,0:T(8,128)(4,1)S(1)} %get-tuple-element.5, f32[]{:T(128)} %bitcast.20, ...), kind=kLoop, calls=%fused_computation.134 | loop fusion | flops 7168 | bytes 8212 | tf_op jit(solution)/shard_map/mul | solution.py:88
  14.9 0.0 collective-permute-done.1
  14.9 0.0 collective-permute-done
  14.9 1.7 %fusion.3 = f32[32,3,3,18,130]{4,0,3,2,1:T(8,128)S(1)} fusion(bf16[32,3,1,16,128]{4,0,3,2,1:T(8,128)(2,1)S(1)} %collective-permute-done.1, bf16[32,3,1,16,128]{4,0,3,2,1:T(8,128)(2,1)S(1)} %multiply_convert_fusion.1, bf16[32,3,1,16,128]{4,0,3,2,1:T(8,128)(2,1)S(1)} %collective-permute-done), kind=kLoop, calls=%fused_computation.8 | loop fusion | flops 12804480 | bytes 3875328 | tf_op jit(solution)/shard_map/jit(_pad)/pad | solution.py:74
  16.6 0.9 %slice_bitcast_fusion = (f32[32,3,18,130]{3,0,2,1:T(8,128)S(1)}, f32[32,3,18,130]{3,0,2,1:T(8,128)S(1)}, f32[32,3,18,130]{3,0,2,1:T(8,128)S(1)}) fusion(f32[32,3,3,18,130]{4,0,3,2,1:T(8,128)S(1)} %fusion.3), kind=kLoop, calls=%fused_computation.13 | loop fusion | bytes 5391360 | tf_op jit(solution)/shard_map/squeeze | solution.py:50
  17.4 0.5 subtract_multiply_fusion.1
  17.9 0.1 fusion.16
  18.0 0.1 fusion.12
  18.1 0.1 fusion.14
  18.3 0.2 subtract_multiply_fusion.4
  18.5 0.2 subtract_add_fusion.4
  18.7 0.3 subtract_add_fusion.2
  19.0 0.1 subtract_add_fusion.5
  19.2 0.2 subtract_multiply_fusion.5
  19.3 0.6 fusion.23
  20.0 0.7 fusion.37
  20.6 0.7 fusion.51
  21.3 0.8 %fusion.8 = bf16[32,3,16,128]{3,0,1,2:T(8,128)(2,1)} fusion(f32[32,1,16,128]{3,0,1,2:T(8,128)S(1)} %fusion.23, f32[32,1,16,128]{3,0,1,2:T(8,128)S(1)} %bitcast.46, f32[32,1,16,128]{3,0,1,2:T(8,128)S(1)} %bitcast.48, f32[16,128]{1,0:T(8,128)S(1)} %get-tuple-element.4), kind=kLoop, calls=%fused_computation.19 | loop fusion | flops 786432 | bytes 1187840 | tf_op jit(solution)/shard_map/convert_element_type | solution.py:76
  22.2 4.2 %all-to-all-start = ((bf16[32,3,16,128]{3,0,1,2:T(8,128)(2,1)}), bf16[32,3,16,128]{3,0,1,2:T(8,128)(2,1)S(1)}, u32[]{:S(2)}, u32[]{:S(2)}) async-start(bf16[32,3,16,128]{3,0,1,2:T(8,128)(2,1)} %fusion.8), calls=%async_computation | async-start | bytes 786432 | tf_op jit(solution)/shard_map/all_to_all | solution.py:80
  26.4 0.1 fusion.7
  26.5 0.9 %copy.22 = bf16[32,3,1,16,128]{4,3,2,1,0:T(8,128)(2,1)} copy(bf16[32,3,1,16,128]{4,0,3,2,1:T(8,128)(2,1)S(1)} %fusion.7) | data formatting | bytes 786432
  27.4 5.1 %all-to-all-done = bf16[32,3,16,128]{3,0,1,2:T(8,128)(2,1)S(1)} async-done(((bf16[32,3,16,128]{3,0,1,2:T(8,128)(2,1)}), bf16[32,3,16,128]{3,0,1,2:T(8,128)(2,1)S(1)}, u32[]{:S(2)}, u32[]{:S(2)}) %all-to-all-start) | async-done | bytes 393248 | tf_op jit(solution)/shard_map/all_to_all | solution.py:80
  32.5 0.2 copy.27
  32.6 0.2 multiply_convert_fusion
  32.8 0.2 reshape.87
  33.0 0.2 convert_element_type.45
  33.1 0.3 fusion.66
  33.4 46.2 %psum.7 = f32[64,64]{1,0:T(8,128)S(1)} all-reduce(f32[64,64]{1,0:T(8,128)S(1)} %fusion.66), channel_id=1, replica_groups=mesh['slab'=16,'vec'=2] {'slab','vec'}, use_global_device_ids=true, to_apply=%region_0.1 | all-reduce | flops 4096 | bytes 32768 | tf_op jit(solution)/shard_map/psum | solution.py:96
  79.6 0.6 dynamic-slice_multiply_fusion
  (1 shorter events, 0.0 us)
Async XLA Ops:
  6.5 8.4 %collective-permute-start.1 = (bf16[32,3,1,16,128]{4,0,3,2,1:T(8,128)(2,1)S(1)}, bf16[32,3,1,16,128]{4,0,3,2,1:T(8,128)(2,1)S(1)}, u32[]{:S(2)}, u32[]{:S(2)}) collective-permute-start(bf16[32,3,1,16,128]{4,0,3,2,1:T(8,128)(2,1)S(1)} %multiply_convert_fusion.1), channel_id=1, source_target_pairs={{2,0},{4,2},{6,4},{8,6},{10,8},{12,10},{14,12},{16,14},{18,16},{20... | collective-permute-start | bytes 1179656 | tf_op jit(solution)/shard_map/ppermute | solution.py:19
  7.8 7.1 %collective-permute-start = (bf16[32,3,1,16,128]{4,0,3,2,1:T(8,128)(2,1)S(1)}, bf16[32,3,1,16,128]{4,0,3,2,1:T(8,128)(2,1)S(1)}, u32[]{:S(2)}, u32[]{:S(2)}) collective-permute-start(bf16[32,3,1,16,128]{4,0,3,2,1:T(8,128)(2,1)S(1)} %multiply_convert_fusion.1), channel_id=1, source_target_pairs={{0,2},{2,4},{4,6},{6,8},{8,10},{10,12},{12,14},{14,16},{16,18},{18... | collective-permute-start | bytes 1179656 | tf_op jit(solution)/shard_map/ppermute | solution.py:16
  22.2 10.3 %all-to-all-start = ((bf16[32,3,16,128]{3,0,1,2:T(8,128)(2,1)}), bf16[32,3,16,128]{3,0,1,2:T(8,128)(2,1)S(1)}, u32[]{:S(2)}, u32[]{:S(2)}) async-start(bf16[32,3,16,128]{3,0,1,2:T(8,128)(2,1)} %fusion.8), calls=%async_computation | async-start | bytes 786432 | tf_op jit(solution)/shard_map/all_to_all | solution.py:80
where the time goes:
time: 80.7 us; the launch traced here: 80.2 us
  blocking collectives  46.2 us (57%)
  other arithmetic  14.1 us (17%)
  starting transfers between devices  8.58 us (11%)
  local copies, waits for them, and re-layouts  5.18 us (6%)
  waiting for transfers between devices  5.07 us (6%)
  between operations  0.83 us (1%)
    psum x1, blocking collectives, shards(): summed_gram = lax.psum(partial_gram, ('slab', 'vec'))  46.2 us
    all_to_all x1, waiting for transfers between devices, shards(): lax.all_to_all(rows_flat, 'vec', split_axis=2, concat_axis=0, tiled=True)  5.06 us
    all_to_all x1, starting transfers between devices, shards(): lax.all_to_all(rows_flat, 'vec', split_axis=2, concat_axis=0, tiled=True)  4.23 us
    mul x1, other arithmetic, shards(): filtered = (gain * summed).astype(jnp.bfloat16)  3.28 us
    ppermute x1, starting transfers between devices, padded_2(): lax.ppermute(lax.slice_in_dim(block, block.shape[dim] - width, None, axis...  3.05 us
    slice x2, local copies, waits for them, and re-layouts, lookup_table(): table[material]  2.92 us
    mul x1, other arithmetic, shards(): weighted = (mass_share * gathered.astype(jnp.float32)).astype(jnp.bfloat16)  2.56 us
    sub x3, other arithmetic, navier(): summed - dilation_modulus * separable(components[source], operations)  1.99 us
  transfers between devices with their start and end apart: 3, of which 1 were waited for; matrix products, arithmetic and copies ran while one was open for 6% of the time, Pallas kernels for 0%

commit v1 on v0

--- a/solution.py
+++ b/solution.py
@@ -93,7 +93,7 @@
         preferred_element_type=jnp.float32,
     )
     unknowns = 3 * filtered.shape[2] * lax.axis_size("slab") * filtered.shape[3] * filtered.shape[4]
-    summed_gram = lax.psum(partial_gram, ("slab", "vec"))
+    summed_gram = jnp.sum(lax.all_gather(partial_gram, ("slab", "vec")), axis=0)
     row_block = lax.dynamic_slice_in_dim(
         summed_gram, lax.axis_index("vec") * group_count, group_count, 0
     )

time: 80.7 us -> 107 us (1.33)
  blocking collectives: 46.2 us -> 72.7 us
    all_gather x0 -> x1, blocking collectives: none -> 72.7 us  [shards(): summed_gram = jnp.sum(lax.all_gather(partial_gram, ('slab', 'vec')), axis=0)]
    psum x1 -> x0, blocking collectives: 46.2 us -> none  [shards(): summed_gram = lax.psum(partial_gram, ('slab', 'vec'))]
  transfers between devices with their start and end apart: 3 -> 3, of which waited for: 1 -> 1; matrix products, arithmetic and copies ran while one was open for 6% -> 5% of each run, Pallas kernels for 0% -> 0%
where the time goes in v1:
time: 107 us
  blocking collectives  72.7 us (68%)
  other arithmetic  14.2 us (13%)
  starting transfers between devices  8.58 us (8%)
  local copies, waits for them, and re-layouts  5.18 us (5%)
  waiting for transfers between devices  5.07 us (5%)
    all_gather x1, blocking collectives, shards(): summed_gram = jnp.sum(lax.all_gather(partial_gram, ('slab', 'vec')), axis=0)  72.7 us
    all_to_all x1, waiting for transfers between devices, shards(): lax.all_to_all(rows_flat, 'vec', split_axis=2, concat_axis=0, tiled=True)  5.06 us
    all_to_all x1, starting transfers between devices, shards(): lax.all_to_all(rows_flat, 'vec', split_axis=2, concat_axis=0, tiled=True)  4.23 us
    mul x1, other arithmetic, shards(): filtered = (gain * summed).astype(jnp.bfloat16)  3.28 us
    ppermute x1, starting transfers between devices, padded_2(): lax.ppermute(lax.slice_in_dim(block, block.shape[dim] - width, None, axis...  3.05 us
    slice x2, local copies, waits for them, and re-layouts, lookup_table(): table[material]  2.92 us
    mul x1, other arithmetic, shards(): weighted = (mass_share * gathered.astype(jnp.float32)).astype(jnp.bfloat16)  2.56 us
  transfers between devices with their start and end apart: 3, of which 1 were waited for; matrix products, arithmetic and copies ran while one was open for 5% of the time, Pallas kernels for 0%

profile of v1, /device:TPU:0, one launch (start us, length us, event | category | flops | bytes accessed | tf_op | source)
XLA Modules:
  0.0 106.8 jit_solution(3243046079019689320)
XLA Ops:
  0.6 1.5 %fusion.65 = (f32[1]{0:T(128)}, f32[1]{0:T(128)}, f32[1]{0:T(128)}, f32[1]{0:T(128)}) fusion(f32[4]{0:T(128)} %param.8), kind=kLoop, calls=%fused_computation.140 | loop fusion | bytes 32 | tf_op jit(solution)/shard_map/slice | solution.py:27
  2.1 3.3 %multiply_bitcast_fusion = (f32[16,128]{1,0:T(8,128)S(1)}, pred[1,16,128]{2,1,0:T(8,128)(4,1)S(1)}, pred[1,16,128]{2,1,0:T(8,128)(4,1)S(1)}, pred[1,16,128]{2,1,0:T(8,128)(4,1)S(1)}, pred[1,16,128]{2,1,0:T(8,128)(4,1)S(1)}) fusion(s32[1,16,128]{2,1,0:T(8,128)} %param.7, f32[]{:T(128)} %bitcast.3, f32[]{:T(128)} %bitcast.2, f32[]{:T(128)} %bitcast.1, ...), kind=kLoop, calls=%fused_computation.133 | loop fusion | flops 28672 | bytes 32784 | tf_op jit(solution)/shard_map/mul | solution.py:76
  5.4 1.1 %multiply_convert_fusion.1 = bf16[32,3,1,16,128]{4,0,3,2,1:T(8,128)(2,1)S(1)} fusion(bf16[32,3,1,16,128]{4,3,2,1,0:T(8,128)(2,1)} %param.5, f32[16,128]{1,0:T(8,128)S(1)} %get-tuple-element.4), kind=kLoop, calls=%fused_computation.21 | loop fusion | flops 589824 | bytes 794624 | tf_op jit(solution)/shard_map/convert_element_type | solution.py:72
  6.5 1.3 %collective-permute-start.1 = (bf16[32,3,1,16,128]{4,0,3,2,1:T(8,128)(2,1)S(1)}, bf16[32,3,1,16,128]{4,0,3,2,1:T(8,128)(2,1)S(1)}, u32[]{:S(2)}, u32[]{:S(2)}) collective-permute-start(bf16[32,3,1,16,128]{4,0,3,2,1:T(8,128)(2,1)S(1)} %multiply_convert_fusion.1), channel_id=1, source_target_pairs={{2,0},{4,2},{6,4},{8,6},{10,8},{12,10},{14,12},{16,14},{18,16},{20... | collective-permute-start | bytes 1179656 | tf_op jit(solution)/shard_map/ppermute | solution.py:19
  7.8 3.1 %collective-permute-start = (bf16[32,3,1,16,128]{4,0,3,2,1:T(8,128)(2,1)S(1)}, bf16[32,3,1,16,128]{4,0,3,2,1:T(8,128)(2,1)S(1)}, u32[]{:S(2)}, u32[]{:S(2)}) collective-permute-start(bf16[32,3,1,16,128]{4,0,3,2,1:T(8,128)(2,1)S(1)} %multiply_convert_fusion.1), channel_id=1, source_target_pairs={{0,2},{2,4},{4,6},{6,8},{8,10},{10,12},{12,14},{14,16},{16,18},{18... | collective-permute-start | bytes 1179656 | tf_op jit(solution)/shard_map/ppermute | solution.py:16
  10.8 1.5 %fusion.64 = (f32[1]{0:T(128)}, f32[1]{0:T(128)}, f32[1]{0:T(128)}, f32[1]{0:T(128)}) fusion(f32[4]{0:T(128)} %param.9), kind=kLoop, calls=%fused_computation.139 | loop fusion | bytes 32 | tf_op jit(solution)/shard_map/slice | solution.py:27
  12.3 2.6 %add_bitcast_fusion = f32[8,128]{1,0:T(8,128)S(1)} fusion(pred[1,16,128]{2,1,0:T(8,128)(4,1)S(1)} %get-tuple-element.8, s32[]{:T(128)S(6)} %select_n.39, pred[1,16,128]{2,1,0:T(8,128)(4,1)S(1)} %get-tuple-element.7, pred[1,16,128]{2,1,0:T(8,128)(4,1)S(1)} %get-tuple-element.6, pred[1,16,128]{2,1,0:T(8,128)(4,1)S(1)} %get-tuple-element.5, f32[]{:T(128)} %bitcast.20, ...), kind=kLoop, calls=%fused_computation.134 | loop fusion | flops 7168 | bytes 8212 | tf_op jit(solution)/shard_map/mul | solution.py:88
  14.9 0.0 collective-permute-done.1
  14.9 0.0 collective-permute-done
  14.9 1.7 %fusion.3 = f32[32,3,3,18,130]{4,0,3,2,1:T(8,128)S(1)} fusion(bf16[32,3,1,16,128]{4,0,3,2,1:T(8,128)(2,1)S(1)} %collective-permute-done.1, bf16[32,3,1,16,128]{4,0,3,2,1:T(8,128)(2,1)S(1)} %multiply_convert_fusion.1, bf16[32,3,1,16,128]{4,0,3,2,1:T(8,128)(2,1)S(1)} %collective-permute-done), kind=kLoop, calls=%fused_computation.8 | loop fusion | flops 12804480 | bytes 3875328 | tf_op jit(solution)/shard_map/jit(_pad)/pad | solution.py:74
  16.6 0.9 slice_bitcast_fusion
  17.4 0.5 subtract_multiply_fusion.1
  17.9 0.1 fusion.16
  18.0 0.1 fusion.12
  18.1 0.1 fusion.14
  18.3 0.2 subtract_multiply_fusion.4
  18.5 0.2 subtract_add_fusion.4
  18.7 0.3 subtract_add_fusion.2
  19.0 0.1 subtract_add_fusion.5
  19.2 0.2 subtract_multiply_fusion.5
  19.3 0.6 fusion.23
  20.0 0.7 fusion.37
  20.6 0.7 fusion.51
  21.3 0.8 fusion.8
  22.2 4.2 %all-to-all-start = ((bf16[32,3,16,128]{3,0,1,2:T(8,128)(2,1)}), bf16[32,3,16,128]{3,0,1,2:T(8,128)(2,1)S(1)}, u32[]{:S(2)}, u32[]{:S(2)}) async-start(bf16[32,3,16,128]{3,0,1,2:T(8,128)(2,1)} %fusion.8), calls=%async_computation | async-start | bytes 786432 | tf_op jit(solution)/shard_map/all_to_all | solution.py:80
  26.4 0.1 fusion.7
  26.5 0.9 copy.22
  27.4 5.1 %all-to-all-done = bf16[32,3,16,128]{3,0,1,2:T(8,128)(2,1)S(1)} async-done(((bf16[32,3,16,128]{3,0,1,2:T(8,128)(2,1)}), bf16[32,3,16,128]{3,0,1,2:T(8,128)(2,1)S(1)}, u32[]{:S(2)}, u32[]{:S(2)}) %all-to-all-start) | async-done | bytes 393248 | tf_op jit(solution)/shard_map/all_to_all | solution.py:80
  32.5 0.2 copy.27
  32.6 0.2 multiply_convert_fusion
  32.8 0.2 reshape.87
  33.0 0.2 convert_element_type.45
  33.1 0.3 fusion.66
  33.4 72.7 %all-gather = f32[2048,64]{1,0:T(8,128)S(1)} all-gather(f32[64,64]{1,0:T(8,128)S(1)} %fusion.66), channel_id=2, replica_groups=mesh['slab'=16,'vec'=2] {'slab','vec'}, dimensions={0}, use_global_device_ids=true | all-gather | bytes 540672 | tf_op jit(solution)/shard_map/all_gather | solution.py:96
  106.1 0.1 reduce_sum.9
  106.2 0.6 dynamic-slice_multiply_fusion
  (1 shorter events, 0.0 us)
Async XLA Ops:
  6.5 8.4 %collective-permute-start.1 = (bf16[32,3,1,16,128]{4,0,3,2,1:T(8,128)(2,1)S(1)}, bf16[32,3,1,16,128]{4,0,3,2,1:T(8,128)(2,1)S(1)}, u32[]{:S(2)}, u32[]{:S(2)}) collective-permute-start(bf16[32,3,1,16,128]{4,0,3,2,1:T(8,128)(2,1)S(1)} %multiply_convert_fusion.1), channel_id=1, source_target_pairs={{2,0},{4,2},{6,4},{8,6},{10,8},{12,10},{14,12},{16,14},{18,16},{20... | collective-permute-start | bytes 1179656 | tf_op jit(solution)/shard_map/ppermute | solution.py:19
  7.8 7.1 %collective-permute-start = (bf16[32,3,1,16,128]{4,0,3,2,1:T(8,128)(2,1)S(1)}, bf16[32,3,1,16,128]{4,0,3,2,1:T(8,128)(2,1)S(1)}, u32[]{:S(2)}, u32[]{:S(2)}) collective-permute-start(bf16[32,3,1,16,128]{4,0,3,2,1:T(8,128)(2,1)S(1)} %multiply_convert_fusion.1), channel_id=1, source_target_pairs={{0,2},{2,4},{4,6},{6,8},{8,10},{10,12},{12,14},{14,16},{16,18},{18... | collective-permute-start | bytes 1179656 | tf_op jit(solution)/shard_map/ppermute | solution.py:16
  22.2 10.3 %all-to-all-start = ((bf16[32,3,16,128]{3,0,1,2:T(8,128)(2,1)}), bf16[32,3,16,128]{3,0,1,2:T(8,128)(2,1)S(1)}, u32[]{:S(2)}, u32[]{:S(2)}) async-start(bf16[32,3,16,128]{3,0,1,2:T(8,128)(2,1)} %fusion.8), calls=%async_computation | async-start | bytes 786432 | tf_op jit(solution)/shard_map/all_to_all | solution.py:80
